TPU v7x, 128 devices: a whole 4x4x4 slice. The times are simulated.
128 devices in a mesh: inp: 8 (over z, x_hi), tm: 8 (over x_lo, y), bl: 2 (over core).
Axes of the slice: x: 4 (x_hi: 2, x_lo: 2; x = x_hi * 2 + x_lo), y: 4, z: 4, core: 2. Of those that a mesh axis runs over, the one named last changes fastest.
Arguments:
- voltages: int32 [1024, 524288], P(('inp', 'bl'), 'tm'), may hold values from -16 to 14, as said below
- taps: float32 [4, 16384], replicated, may hold values from -3 to 3
- flags: int32 [1024], P(('inp', 'bl')), may hold values 0 or 1
Outputs:
- visibilities: float32 [2, 128, 8, 128, 1024], P(None, ('inp', 'tm'), None, 'bl')
Inputs may be any that keep to these rules, and one draw needn't show every extreme that they name: `voltages`: int8-valued digitized samples, each input's stream in time order.
All inputs are finite; a program needn't handle non-finite values. No bound on the sum of `flags` on one device may be relied on, other than what follows from the above.
Results may differ from a plain program's by a relative error of at most 0.00065.
Values may be sent and summed in bfloat16 or wider, within the bound.
A program may use at most 192 MiB of HBM per device.

v0:
```python
import math
import jax
import jax.numpy as jnp
from jax import lax
from jax.sharding import PartitionSpec as P

CH_AVG = 64


def passed_along(value, axis, steps):
    count = lax.axis_size(axis)
    initial, last = (max(0, -steps), min(count, count - steps))
    return lax.ppermute(value, axis, [(source, source + steps) for source in range(initial, last)])


def cos_sin(height, breadth, period):
    grid = lax.broadcasted_iota(jnp.int32, (height, breadth), 0) * lax.broadcasted_iota(
        jnp.int32, (height, breadth), 1
    )
    angle = (grid % period).astype(jnp.float32) * (2.0 * math.pi / period)
    return (jnp.cos(angle), jnp.sin(angle))


def transform(filtered, length):
    batch = filtered.shape[0]
    first_len = 128
    second_len = length // first_len
    highest = lax.Precision.HIGHEST
    blocks = filtered.reshape(batch, first_len, second_len)
    cos_one, sin_one = cos_sin(first_len, first_len, first_len)
    table_one = jnp.stack([cos_one, -sin_one])
    section_one = jnp.einsum("ykn,mnb->mykb", table_one, blocks, precision=highest)
    cos_twist, sin_twist = cos_sin(first_len, second_len, length)
    real_one = section_one[:, 0]
    imag_one = section_one[:, 1]
    twisted = jnp.stack(
        [real_one * cos_twist + imag_one * sin_twist, imag_one * cos_twist - real_one * sin_twist],
        axis=1,
    )
    cos_two, sin_two = cos_sin(second_len, second_len // 2, second_len)
    table_two = jnp.stack(
        [jnp.stack([cos_two, -sin_two], axis=1), jnp.stack([sin_two, cos_two], axis=1)]
    )
    result = jnp.einsum("mxkb,xbyq->ymqk", twisted, table_two, precision=highest)
    return result.reshape(2, batch, length // 2)


def shards(voltages, taps, flags):
    inputs = voltages.shape[0]
    tap_count = taps.shape[0]
    length = taps.shape[1]
    spectra_dev = voltages.shape[1] // length
    reach = tap_count - 1
    samples = voltages.astype(jnp.float32).reshape(inputs, spectra_dev, length)
    leading = voltages[:, : reach * length].reshape(inputs, reach, length).astype(jnp.bfloat16)
    following = passed_along(leading, "tm", -1)
    extended = jnp.concatenate([samples, following.astype(jnp.float32)], axis=1)
    filtered = jnp.zeros((inputs, spectra_dev, length), jnp.float32)
    for offset in range(tap_count):
        filtered = (
            filtered + taps[offset][None, None, :] * extended[:, offset : offset + spectra_dev]
        )
    channels = length // 2
    both_parts = transform(filtered.reshape(inputs * spectra_dev, length), length)
    scale = flags.astype(jnp.float32)[None, :, None, None] / (8.0 * math.sqrt(length))
    spectra = (both_parts.reshape(2, inputs, spectra_dev, channels) * scale).astype(jnp.bfloat16)
    turned = lax.all_to_all(
        spectra[:, None], ("inp", "tm"), split_axis=4, concat_axis=1, tiled=True
    )
    groups_inp = lax.axis_size("inp")
    groups_tm = lax.axis_size("tm")
    local_channels = channels // (groups_inp * groups_tm)
    out_groups = local_channels // CH_AVG
    rows = turned.reshape(2, groups_inp, groups_tm, inputs, spectra_dev, out_groups, CH_AVG)
    count = float(groups_tm * spectra_dev * CH_AVG)
    products = jnp.einsum(
        "xatisgk,yctjsgk->gxyaicj",
        rows,
        lax.all_gather(rows, "bl", axis=3, tiled=True),
        preferred_element_type=jnp.float32,
    )
    real_vis = products[:, 0, 0] + products[:, 1, 1]
    imag_vis = products[:, 1, 0] - products[:, 0, 1]
    visibilities = jnp.stack([real_vis, imag_vis]) / count
    return visibilities.reshape(
        2, out_groups, groups_inp, inputs, groups_inp * inputs * lax.axis_size("bl")
    )


def solution(mesh):
    in_specs = (P(("inp", "bl"), "tm"), P(), P(("inp", "bl")))
    out_specs = P(None, ("inp", "tm"), None, "bl", None)
    return jax.shard_map(shards, mesh=mesh, in_specs=in_specs, out_specs=out_specs, check_vma=False)
```

profile of v0, /device:TPU:1, one launch (start us, length us, event | category | flops | bytes accessed | tf_op | source)
XLA Modules:
  0.0 725.3 jit_solution(16236080894492939012)
XLA Ops:
  6.5 0.0 all-gather.2.cloned.1.call-start
  6.5 5.2 slice_convert_fusion
  11.8 3.1 copy.89
  14.9 1.3 collective-permute-start
  16.2 11.3 %convert_element_type.80 = f32[64,65536]{1,0:T(8,128)} convert(s32[64,65536]{1,0:T(8,128)} %param.3) | non-fusion elementwise | flops 4194304 | bytes 33554432 | tf_op jit(solution)/shard_map/convert_element_type | solution.py:54
  27.5 0.0 copy-start.2
  27.5 0.0 copy-start.1
  27.5 17.6 %reshape.218 = f32[64,4,16384]{2,1,0:T(4,128)} reshape(f32[64,65536]{1,0:T(8,128)} %convert_element_type.80) | data formatting | bytes 33554432 | tf_op jit(solution)/shard_map/reshape | solution.py:54
  45.1 0.0 copy-start
  45.1 0.1 fusion.53
  45.2 0.1 fusion.51
  45.4 0.3 sine_negate_fusion
  45.6 0.3 fusion.45
  45.9 0.0 copy-done.2
  46.0 0.0 copy-done.1
  46.0 0.2 fusion.56
  46.2 107.9 %collective-permute-done = bf16[64,3,16384]{2,0,1:T(8,128)(2,1)} collective-permute-done((bf16[64,3,16384]{2,0,1:T(8,128)(2,1)}, bf16[64,3,16384]{2,0,1:T(8,128)(2,1)}, u32[]{:S(2)}, u32[]{:S(2)}) %collective-permute-start) | collective-permute-done | bytes 6291488 | tf_op jit(solution)/shard_map/ppermute | solution.py:13
  154.1 11.2 %copy.53 = f32[64,3,16384]{2,1,0:T(4,128)} copy(bf16[64,3,16384]{2,0,1:T(8,128)(2,1)} %collective-permute-done) | data formatting | bytes 18874368 | tf_op jit(solution)/shard_map/convert_element_type | solution.py:57
  165.3 0.0 copy-done
  165.3 32.6 %fusion.8 = f32[64,4,16384]{2,1,0:T(4,128)} fusion(f32[64,4,16384]{2,1,0:T(4,128)S(1)} %copy-done, f32[64,3,16384]{2,1,0:T(4,128)} %copy.53, f32[16384]{0:T(1024)S(1)} %bitcast.77, f32[16384]{0:T(1024)S(1)} %bitcast.78, f32[16384]{0:T(1024)S(1)} %bitcast.76, f32[16384]{0:T(1024)S(1)} %bitcast.75), kind=kLoop, calls=%fused_computation.13 | loop fusion | flops 41943040 | bytes 46399488 | tf_op jit(solution)/shard_map/add | solution.py:61
  197.9 20.5 %reshape_reshape.6 = f32[256,128,128]{2,1,0:T(8,128)} reshape(f32[64,4,16384]{2,1,0:T(4,128)} %fusion.8) | data formatting | bytes 33554432 | tf_op jit(solution)/shard_map/reshape;reshape | solution.py:29
  218.4 32.5 %fusion.17 = f32[256,2,128,128]{2,3,1,0:T(8,128)} fusion(f32[256,128,128]{2,1,0:T(8,128)} %reshape_reshape.6, f32[1,128,128]{2,1,0:T(8,128)S(1)} %get-tuple-element.15, f32[1,128,128]{2,1,0:T(8,128)S(1)} %get-tuple-element.16), kind=kOutput, calls=%fused_computation.26 | convolution fusion | flops 12884934656 | bytes 50462720 | tf_op jit(solution)/shard_map/ykn,mnb->mykb/dot_general | solution.py:32
  250.8 17.8 %multiply_add_fusion = (f32[256,1,128,128]{2,3,1,0:T(8,128)S(1)}, f32[256,1,128,128]{2,3,1,0:T(8,128)}) fusion(f32[256,2,128,128]{2,3,1,0:T(8,128)} %fusion.17, f32[128,128]{0,1:T(8,128)S(1)} %get-tuple-element.17, f32[128,128]{0,1:T(8,128)S(1)} %get-tuple-element.18), kind=kLoop, calls=%fused_computation.25 | loop fusion | flops 25165824 | bytes 67239936 | tf_op jit(solution)/shard_map/add | solution.py:37
  268.6 23.6 %fusion.25 = f32[2,256,64,128]{3,2,1,0:T(8,128)} fusion(f32[256,1,128,128]{2,3,1,0:T(8,128)} %get-tuple-element.6, f32[256,1,128,128]{2,3,1,0:T(8,128)S(1)} %get-tuple-element.5, f32[1,128,2,64]{1,3,0,2:T(8,128)S(1)} %get-tuple-element.14, f32[1,128,2,64]{1,3,0,2:T(8,128)S(1)} %get-tuple-element.13), kind=kOutput, calls=%fused_computation.30 | convolution fusion | flops 12893323264 | bytes 50462720 | tf_op jit(solution)/shard_map/mxkb,xbyq->ymqk/dot_general | solution.py:44
  292.2 19.9 %reshape_reshape.7 = f32[2,1,64,4,8192]{4,3,2,0,1:T(4,128)} reshape(f32[2,256,64,128]{3,2,1,0:T(8,128)} %fusion.25) | data formatting | bytes 33554432 | tf_op jit(solution)/shard_map/reshape;reshape | solution.py:66
  312.2 16.6 %fusion.16 = bf16[2,1,64,4,8192]{4,2,3,1,0:T(8,128)(2,1)} fusion(f32[2,1,64,4,8192]{4,3,2,0,1:T(4,128)} %reshape_reshape.7, f32[64]{0:T(128)S(1)} %convert_multiply_fusion), kind=kLoop, calls=%fused_computation.23 | loop fusion | flops 8388608 | bytes 25166080 | tf_op jit(solution)/shard_map/convert_element_type | solution.py:66
  328.8 24.4 %copy.57 = bf16[2,1,64,4,8192]{2,3,0,1,4:T(4,128)(2,1)} copy(bf16[2,1,64,4,8192]{4,2,3,1,0:T(8,128)(2,1)} %fusion.16) | data formatting | bytes 16777216 | tf_op jit(solution)/shard_map/convert_element_type | solution.py:66
  353.2 26.5 %reshape.228 = bf16[64,2,32768]{2,1,0:T(2,128)(2,1)} reshape(bf16[8192,1,2,4,64]{4,3,2,1,0:T(4,128)(2,1)} %bitcast.68) | data formatting | bytes 16777216
  379.7 108.5 %all_to_all.15 = bf16[64,2,32768]{2,1,0:T(2,128)(2,1)} all-to-all(bf16[64,2,32768]{2,1,0:T(2,128)(2,1)} %reshape.228), channel_id=1, replica_groups=mesh['inp'=8,'tm'=8,'bl'=2] {'inp','tm'}, dimensions={0} | all-to-all | bytes 16777216 | tf_op jit(solution)/shard_map/all_to_all | solution.py:67
  488.2 26.0 %reshape.229 = bf16[8192,1,2,4,64]{4,3,2,1,0:T(4,128)(2,1)} reshape(bf16[64,2,32768]{2,1,0:T(2,128)(2,1)} %all_to_all.15) | data formatting | bytes 16777216
  514.2 23.4 %copy.77 = bf16[2,1,64,4,64,128]{5,2,3,4,0,1:T(8,128)(2,1)} copy(bf16[2,1,64,4,64,128]{2,3,0,5,4,1:T(4,128)(2,1)} %bitcast.69) | data formatting | bytes 16777216 | tf_op jit(solution)/shard_map/all_to_all | solution.py:67
  537.6 27.8 %reshape.219 = bf16[2,8,8,64,4,2,64]{6,5,3,4,2,1,0:T(2,128)(2,1)} reshape(bf16[2,64,1,64,4,128]{5,3,4,1,0,2:T(8,128)(2,1)} %bitcast.71) | data formatting | bytes 16777216 | tf_op jit(solution)/shard_map/reshape | solution.py:74
  565.4 15.2 %copy.60 = bf16[2,8,8,64,4,2,64]{6,3,2,4,1,0,5:T(8,128)(2,1)} copy(bf16[2,8,8,64,4,2,64]{6,5,3,4,2,1,0:T(2,128)(2,1)} %reshape.219) | data formatting | bytes 16777216 | tf_op jit(solution)/shard_map/reshape | solution.py:74
  580.6 0.0 all-gather.2.cloned.1.call-update
  580.6 54.9 %all-gather.2.cloned.1.call-done = bf16[2,8,8,128,4,2,64]{6,3,2,4,1,0,5:T(8,128)(2,1)} async-done(((bf16[2,8,8,64,4,2,64]{6,3,2,4,1,0,5:T(8,128)(2,1)}), bf16[2,8,8,128,4,2,64]{6,3,2,4,1,0,5:T(8,128)(2,1)}) %all-gather.2.cloned.1.call-update) | async-done | bytes 16777232 | tf_op jit(solution)/shard_map/all_gather | solution.py:79
  635.4 57.3 %fusion.20 = f32[2,2,2,8,64,8,128]{6,4,3,1,5,2,0:T(8,128)} fusion(bf16[2,8,8,64,4,2,64,1,1]{6,5,3,4,2,1,0,8,7:T(2,128)(2,1)} %bitcast.70, bf16[2,8,8,128,4,2,64]{6,3,2,4,1,0,5:T(8,128)(2,1)} %all-gather.2.cloned.1.call-done), kind=kOutput, calls=%fused_computation.29 | convolution fusion | flops 17179869184 | bytes 41943040 | tf_op jit(solution)/shard_map/xatisgk,yctjsgk->gxyaicj/dot_general | solution.py:76
  692.8 10.4 %slice_add_fusion = (f32[2,1,1,8,64,8,128]{6,4,3,1,5,2,0:T(8,128)}, f32[2,1,1,8,64,8,128]{6,4,3,1,5,2,0:T(8,128)S(1)}) fusion(f32[2,2,2,8,64,8,128]{6,4,3,1,5,2,0:T(8,128)} %fusion.20), kind=kLoop, calls=%fused_computation.33 | loop fusion | flops 2097152 | bytes 25165824 | tf_op jit(solution)/shard_map/add | solution.py:82
  703.1 5.5 copy.62
  708.6 1.0 copy.64
  709.6 3.3 copy.63
  712.9 1.0 copy.65
  713.9 4.4 maximum_multiply_fusion
  (2 shorter events, 0.0 us)
Async XLA Ops:
  6.5 628.9 %all-gather.2.cloned.1.call-start = ((), (), s32[]{:S(2)}) async-start(), calls=%async_computation.1 | async-start | bytes 50331648 | tf_op jit(solution)/shard_map/all_gather | solution.py:79
  14.9 139.2 %collective-permute-start = (bf16[64,3,16384]{2,0,1:T(8,128)(2,1)}, bf16[64,3,16384]{2,0,1:T(8,128)(2,1)}, u32[]{:S(2)}, u32[]{:S(2)}) collective-permute-start(bf16[64,3,16384]{2,0,1:T(8,128)(2,1)} %bitcast.67), channel_id=1, source_target_pairs={{2,0},{4,2},{6,4},{8,6},{10,8},{12,10},{14,12},{3,1},{5,3},{7,5},{... | collective-permute-start | bytes 18874376 | tf_op jit(solution)/shard_map/ppermute | solution.py:13
  27.5 18.5 %copy-start.2 = (s32[64]{0:T(128)S(1)}, s32[64]{0:T(128)}, u32[]{:S(2)}) copy-start(s32[64]{0:T(128)} %param.5) | copy-start | bytes 772
  27.5 18.5 %copy-start.1 = (f32[4,16384]{1,0:T(4,128)S(1)}, f32[4,16384]{1,0:T(4,128)}, u32[]{:S(2)}) copy-start(f32[4,16384]{1,0:T(4,128)} %param.4) | copy-start | bytes 786436
  45.1 120.2 %copy-start = (f32[64,4,16384]{2,1,0:T(4,128)S(1)}, f32[64,4,16384]{2,1,0:T(4,128)}, u32[]{:S(2)}) copy-start(f32[64,4,16384]{2,1,0:T(4,128)} %reshape.218) | copy-start | bytes 50331652
Sparse Core Ops, SparseCore 0:
  580.7 54.6 all-gather.1
where the time goes:
time: 737 us; the launch traced here: 725 us
  local copies, waits for them, and re-layouts  227 us (31%)
  waiting for transfers between devices  163 us (22%)
  matrix products  113 us (15%)
  blocking collectives  108 us (15%)
  other arithmetic  99 us (13%)
  between operations  13.7 us (2%)
    all_to_all x1, blocking collectives, shards(): lax.all_to_all(spectra[:, None], ('inp', 'tm'), split_axis=4, concat_axis...  108 us
    ppermute x1, waiting for transfers between devices, passed_along(): lax.ppermute(value, axis, [(source, source + steps) for source in range(i...  108 us
    dot_general x1, matrix products, shards(): jnp.einsum('xatisgk,yctjsgk->gxyaicj', rows, lax.all_gather(rows, 'bl', a...  57.3 us
    all_gather x1, waiting for transfers between devices, shards(): lax.all_gather(rows, 'bl', axis=3, tiled=True)  54.9 us
    unnamed x8, local copies, waits for them, and re-layouts  52.6 us
    reshape x2, local copies, waits for them, and re-layouts, shards(): turned.reshape(2, groups_inp, groups_tm, inputs, spectra_dev, out_groups,...  43 us
    add x1, other arithmetic, shards(): filtered + taps[offset][None, None, :] * extended[:, offset:offset + spec...  32.6 us
    dot_general x1, matrix products, transform(): jnp.einsum('ykn,mnb->mykb', table_one, blocks, precision=highest)  32.5 us
  transfers between devices with their start and end apart: 2, of which 2 were waited for; matrix products, arithmetic and copies ran while one was open for 4% of the time, Pallas kernels for 0%

commit v1 on v0

--- a/solution.py
+++ b/solution.py
@@ -1,3 +1,4 @@
+import functools
 import math
 import jax
 import jax.numpy as jnp
@@ -5,6 +6,18 @@
 from jax.sharding import PartitionSpec as P
 
 CH_AVG = 64
+
+
+def group_heaps(unit, across):
+    return jnp.concatenate(
+        jax.lax.all_to_all(
+            jnp.stack(jnp.split(unit, jax.lax.axis_size(across), 4), 0), across, 0, 0
+        ),
+        1,
+    )
+
+
+leaves_scan = functools.partial(group_heaps, across=("inp", "tm"))
 
 
 def passed_along(value, axis, steps):
@@ -64,9 +77,7 @@
     both_parts = transform(filtered.reshape(inputs * spectra_dev, length), length)
     scale = flags.astype(jnp.float32)[None, :, None, None] / (8.0 * math.sqrt(length))
     spectra = (both_parts.reshape(2, inputs, spectra_dev, channels) * scale).astype(jnp.bfloat16)
-    turned = lax.all_to_all(
-        spectra[:, None], ("inp", "tm"), split_axis=4, concat_axis=1, tiled=True
-    )
+    turned = leaves_scan(spectra[:, None])
     groups_inp = lax.axis_size("inp")
     groups_tm = lax.axis_size("tm")
     local_channels = channels // (groups_inp * groups_tm)

time: 737 us -> 647 us (0.88)
  local copies, waits for them, and re-layouts: 227 us -> 140 us
    unnamed x8 -> x69, local copies, waits for them, and re-layouts: 52.6 us -> 3.12 us
    another operation x0 -> x3, local copies, waits for them, and re-layouts: none -> 43 us  [the longest x2 43 us: shards(): turned.reshape(2, groups_inp, groups_tm, inputs, spectra_dev, out_groups,...]
    reshape x2 -> x1, local copies, waits for them, and re-layouts: 43 us -> 10.7 us  [group_heaps(): jnp.concatenate(jax.lax.all_to_all(jnp.stack(jnp.split(unit, jax.lax.axis...]
    convert_element_type x1 -> x0, local copies, waits for them, and re-layouts: 24.4 us -> none  [shards(): (both_parts.reshape(2, inputs, spectra_dev, channels) * scale).astype(jnp...]
    all_to_all x1 -> x0, local copies, waits for them, and re-layouts: 23.4 us -> none  [shards(): lax.all_to_all(spectra[:, None], ('inp', 'tm'), split_axis=4, concat_axis...]
  transfers between devices with their start and end apart: 2 -> 2, of which waited for: 2 -> 2; matrix products, arithmetic and copies ran while one was open for 4% -> 5% of each run, Pallas kernels for 0% -> 0%
where the time goes in v1:
time: 647 us; the launch traced here: 638 us
  waiting for transfers between devices  163 us (25%)
  local copies, waits for them, and re-layouts  140 us (22%)
  matrix products  113 us (17%)
  blocking collectives  108 us (17%)
  other arithmetic  97.7 us (15%)
  between operations  14 us (2%)
    ppermute x1, waiting for transfers between devices, passed_along(): lax.ppermute(value, axis, [(source, source + steps) for source in range(i...  108 us
    all_to_all x1, blocking collectives, group_heaps(): jax.lax.all_to_all(jnp.stack(jnp.split(unit, jax.lax.axis_size(across), 4...  108 us
    dot_general x1, matrix products, shards(): jnp.einsum('xatisgk,yctjsgk->gxyaicj', rows, lax.all_gather(rows, 'bl', a...  57.3 us
    all_gather x1, waiting for transfers between devices, shards(): lax.all_gather(rows, 'bl', axis=3, tiled=True)  55.3 us
    another operation x2, local copies, waits for them, and re-layouts, shards(): turned.reshape(2, groups_inp, groups_tm, inputs, spectra_dev, out_groups,...  43 us
    add x1, other arithmetic, shards(): filtered + taps[offset][None, None, :] * extended[:, offset:offset + spec...  32.6 us
    dot_general x1, matrix products, transform(): jnp.einsum('ykn,mnb->mykb', table_one, blocks, precision=highest)  32.5 us
    dot_general x1, matrix products, transform(): jnp.einsum('mxkb,xbyq->ymqk', twisted, table_two, precision=highest)  23.6 us
  transfers between devices with their start and end apart: 2, of which 2 were waited for; matrix products, arithmetic and copies ran while one was open for 5% of the time, Pallas kernels for 0%

profile of v1, /device:TPU:1, one launch (start us, length us, event | category | flops | bytes accessed | tf_op | source)
XLA Modules:
  0.0 637.6 jit_solution(7686779403682112064)
XLA Ops:
  6.5 5.2 slice_convert_fusion
  11.8 3.1 copy.124
  14.9 1.3 collective-permute-start
  16.2 11.3 %convert_element_type.80 = f32[64,65536]{1,0:T(8,128)} convert(s32[64,65536]{1,0:T(8,128)} %param.3) | non-fusion elementwise | flops 4194304 | bytes 33554432 | tf_op jit(solution)/shard_map/convert_element_type | solution.py:67
  27.5 17.6 %reshape.217 = f32[64,4,16384]{2,1,0:T(4,128)} reshape(f32[64,65536]{1,0:T(8,128)} %convert_element_type.80) | data formatting | bytes 33554432 | tf_op jit(solution)/shard_map/reshape | solution.py:67
  45.1 0.1 fusion.53
  45.2 0.1 fusion.51
  45.4 0.3 sine_negate_fusion
  45.6 0.3 fusion.45
  46.0 0.2 fusion.56
  46.2 107.9 %collective-permute-done = bf16[64,3,16384]{2,0,1:T(8,128)(2,1)} collective-permute-done((bf16[64,3,16384]{2,0,1:T(8,128)(2,1)}, bf16[64,3,16384]{2,0,1:T(8,128)(2,1)}, u32[]{:S(2)}, u32[]{:S(2)}) %collective-permute-start) | collective-permute-done | bytes 6291488 | tf_op jit(solution)/shard_map/ppermute | solution.py:26
  154.1 11.2 %copy.92 = f32[64,3,16384]{2,1,0:T(4,128)} copy(bf16[64,3,16384]{2,0,1:T(8,128)(2,1)} %collective-permute-done) | data formatting | bytes 18874368 | tf_op jit(solution)/shard_map/convert_element_type | solution.py:70
  165.3 32.6 %fusion.8 = f32[64,4,16384]{2,1,0:T(4,128)} fusion(f32[64,4,16384]{2,1,0:T(4,128)S(1)} %copy-done, f32[64,3,16384]{2,1,0:T(4,128)} %copy.92, f32[16384]{0:T(1024)S(1)} %bitcast.327, f32[16384]{0:T(1024)S(1)} %bitcast.328, f32[16384]{0:T(1024)S(1)} %bitcast.326, f32[16384]{0:T(1024)S(1)} %bitcast.325), kind=kLoop, calls=%fused_computation.13 | loop fusion | flops 41943040 | bytes 46399488 | tf_op jit(solution)/shard_map/add | solution.py:74
  197.9 20.5 %reshape_reshape.9 = f32[256,128,128]{2,1,0:T(8,128)} reshape(f32[64,4,16384]{2,1,0:T(4,128)} %fusion.8) | data formatting | bytes 33554432 | tf_op jit(solution)/shard_map/reshape;reshape | solution.py:42
  218.4 32.5 %fusion.17 = f32[256,2,128,128]{2,3,1,0:T(8,128)} fusion(f32[256,128,128]{2,1,0:T(8,128)} %reshape_reshape.9, f32[1,128,128]{2,1,0:T(8,128)S(1)} %get-tuple-element.15, f32[1,128,128]{2,1,0:T(8,128)S(1)} %get-tuple-element.16), kind=kOutput, calls=%fused_computation.26 | convolution fusion | flops 12884934656 | bytes 50462720 | tf_op jit(solution)/shard_map/ykn,mnb->mykb/dot_general | solution.py:45
  250.8 17.8 %multiply_add_fusion = (f32[256,1,128,128]{2,3,1,0:T(8,128)S(1)}, f32[256,1,128,128]{2,3,1,0:T(8,128)}) fusion(f32[256,2,128,128]{2,3,1,0:T(8,128)} %fusion.17, f32[128,128]{0,1:T(8,128)S(1)} %get-tuple-element.17, f32[128,128]{0,1:T(8,128)S(1)} %get-tuple-element.18), kind=kLoop, calls=%fused_computation.25 | loop fusion | flops 25165824 | bytes 67239936 | tf_op jit(solution)/shard_map/add | solution.py:50
  268.6 23.6 %fusion.25 = f32[2,256,64,128]{3,2,1,0:T(8,128)} fusion(f32[256,1,128,128]{2,3,1,0:T(8,128)} %get-tuple-element.6, f32[256,1,128,128]{2,3,1,0:T(8,128)S(1)} %get-tuple-element.5, f32[1,128,2,64]{1,3,0,2:T(8,128)S(1)} %get-tuple-element.14, f32[1,128,2,64]{1,3,0,2:T(8,128)S(1)} %get-tuple-element.13), kind=kOutput, calls=%fused_computation.30 | convolution fusion | flops 12893323264 | bytes 50462720 | tf_op jit(solution)/shard_map/mxkb,xbyq->ymqk/dot_general | solution.py:57
  292.2 19.9 %reshape_reshape.10 = f32[2,1,64,4,8192]{4,3,2,0,1:T(4,128)} reshape(f32[2,256,64,128]{3,2,1,0:T(8,128)} %fusion.25) | data formatting | bytes 33554432 | tf_op jit(solution)/shard_map/reshape;reshape | solution.py:79
  312.2 15.3 %fusion.16 = bf16[2,1,64,4,8192]{4,2,3,0,1:T(8,128)(2,1)S(1)} fusion(f32[2,1,64,4,8192]{4,3,2,0,1:T(4,128)} %reshape_reshape.10, f32[64]{0:T(128)S(1)} %convert_multiply_fusion), kind=kLoop, calls=%fused_computation.23 | loop fusion | flops 8388608 | bytes 25166080 | tf_op jit(solution)/shard_map/convert_element_type | solution.py:79
  327.5 0.1 constant_dynamic-update-slice_fusion.62
  327.7 0.1 constant_dynamic-update-slice_fusion.57
  327.8 0.1 constant_dynamic-update-slice_fusion.56
  328.2 0.1 constant_dynamic-update-slice_fusion.49
  328.2 0.1 constant_dynamic-update-slice_fusion.48
  328.6 0.1 constant_dynamic-update-slice_fusion.41
  328.7 0.1 constant_dynamic-update-slice_fusion.40
  329.0 0.1 constant_dynamic-update-slice_fusion.33
  329.1 0.1 constant_dynamic-update-slice_fusion.32
  329.5 0.1 constant_dynamic-update-slice_fusion.25
  329.5 0.1 constant_dynamic-update-slice_fusion.24
  329.9 0.1 constant_dynamic-update-slice_fusion.17
  330.0 0.1 constant_dynamic-update-slice_fusion.16
  330.3 0.1 constant_dynamic-update-slice_fusion.9
  330.4 0.1 constant_dynamic-update-slice_fusion.8
  330.8 0.1 constant_dynamic-update-slice_fusion.1
  330.8 0.1 constant_dynamic-update-slice_fusion
  330.9 107.9 %all_to_all.5 = bf16[64,2,1,64,4,128]{5,3,4,1,2,0:T(8,128)(2,1)} all-to-all(bf16[64,2,1,64,4,128]{5,3,4,1,2,0:T(8,128)(2,1)S(1)} %constant_dynamic-update-slice_fusion), channel_id=1, replica_groups=mesh['inp'=8,'tm'=8,'bl'=2] {'inp','tm'}, dimensions={0} | all-to-all | bytes 16777216 | tf_op jit(solution)/shard_map/all_to_all | solution.py:13
  438.7 10.7 %copy.96 = bf16[2,64,1,64,4,128]{5,3,4,1,0,2:T(8,128)(2,1)} copy(bf16[2,64,1,64,4,128]{5,3,4,0,2,1:T(8,128)(2,1)} %bitcast.321) | data formatting | bytes 16777216 | tf_op jit(solution)/shard_map/reshape | solution.py:12
  449.4 27.8 %reshape_reshape.11 = bf16[2,8,8,64,4,2,64]{6,5,3,4,2,1,0:T(2,128)(2,1)} reshape(bf16[2,64,1,64,4,128]{5,3,4,1,0,2:T(8,128)(2,1)} %copy.96) | data formatting | bytes 16777216 | tf_op jit(solution)/shard_map/reshape;reshape | solution.py:85
  477.2 15.2 %copy.97 = bf16[2,8,8,64,4,2,64]{6,3,2,4,1,0,5:T(8,128)(2,1)} copy(bf16[2,8,8,64,4,2,64]{6,5,3,4,2,1,0:T(2,128)(2,1)} %reshape_reshape.11) | data formatting | bytes 16777216 | tf_op jit(solution)/shard_map/reshape;reshape | solution.py:85
  492.4 55.3 %all-gather.2.cloned.1.call-done = bf16[2,8,8,128,4,2,64]{6,3,2,4,1,0,5:T(8,128)(2,1)} async-done(((bf16[2,8,8,64,4,2,64]{6,3,2,4,1,0,5:T(8,128)(2,1)}), bf16[2,8,8,128,4,2,64]{6,3,2,4,1,0,5:T(8,128)(2,1)}) %all-gather.2.cloned.1.call-update) | async-done | bytes 16777232 | tf_op jit(solution)/shard_map/all_gather | solution.py:90
  547.7 57.3 %fusion.20 = f32[2,2,2,8,64,8,128]{6,4,3,1,5,2,0:T(8,128)} fusion(bf16[2,8,8,64,4,2,64,1,1]{6,5,3,4,2,1,0,8,7:T(2,128)(2,1)} %bitcast.320, bf16[2,8,8,128,4,2,64]{6,3,2,4,1,0,5:T(8,128)(2,1)} %all-gather.2.cloned.1.call-done), kind=kOutput, calls=%fused_computation.29 | convolution fusion | flops 17179869184 | bytes 41943040 | tf_op jit(solution)/shard_map/xatisgk,yctjsgk->gxyaicj/dot_general | solution.py:87
  605.0 10.4 %slice_add_fusion = (f32[2,1,1,8,64,8,128]{6,4,3,1,5,2,0:T(8,128)}, f32[2,1,1,8,64,8,128]{6,4,3,1,5,2,0:T(8,128)S(1)}) fusion(f32[2,2,2,8,64,8,128]{6,4,3,1,5,2,0:T(8,128)} %fusion.20), kind=kLoop, calls=%fused_computation.33 | loop fusion | flops 2097152 | bytes 25165824 | tf_op jit(solution)/shard_map/add | solution.py:93
  615.4 5.5 copy.99
  620.9 1.0 copy.101
  621.9 3.3 copy.100
  625.2 1.0 copy.102
  626.2 4.4 maximum_multiply_fusion
  (57 shorter events, 2.3 us)
Async XLA Ops:
  6.5 541.2 %all-gather.2.cloned.1.call-start = ((), (), s32[]{:S(2)}) async-start(), calls=%async_computation.1 | async-start | bytes 50331648 | tf_op jit(solution)/shard_map/all_gather | solution.py:90
  14.9 139.2 %collective-permute-start = (bf16[64,3,16384]{2,0,1:T(8,128)(2,1)}, bf16[64,3,16384]{2,0,1:T(8,128)(2,1)}, u32[]{:S(2)}, u32[]{:S(2)}) collective-permute-start(bf16[64,3,16384]{2,0,1:T(8,128)(2,1)} %bitcast.319), channel_id=1, source_target_pairs={{2,0},{4,2},{6,4},{8,6},{10,8},{12,10},{14,12},{3,1},{5,3},{7,5},{... | collective-permute-start | bytes 18874376 | tf_op jit(solution)/shard_map/ppermute | solution.py:26
  27.5 18.5 %copy-start.2 = (s32[64]{0:T(128)S(1)}, s32[64]{0:T(128)}, u32[]{:S(2)}) copy-start(s32[64]{0:T(128)} %param.5) | copy-start | bytes 772
  27.5 18.5 %copy-start.1 = (f32[4,16384]{1,0:T(4,128)S(1)}, f32[4,16384]{1,0:T(4,128)}, u32[]{:S(2)}) copy-start(f32[4,16384]{1,0:T(4,128)} %param.4) | copy-start | bytes 786436
  46.2 119.1 %copy-start = (f32[64,4,16384]{2,1,0:T(4,128)S(1)}, f32[64,4,16384]{2,1,0:T(4,128)}, u32[]{:S(2)}) copy-start(f32[64,4,16384]{2,1,0:T(4,128)} %reshape.217) | copy-start | bytes 50331652
Sparse Core Ops, SparseCore 0:
  492.6 55.1 all-gather.1
